TPU v7x, 128 devices: a whole 4x4x4 slice. The times are simulated.
128 devices in a mesh: blk: 16 (over z, x_hi, core), narrow: 8 (over x_lo, y).
Axes of the slice: x: 4 (x_hi: 2, x_lo: 2; x = x_hi * 2 + x_lo), y: 4, z: 4, core: 2. Of those that a mesh axis runs over, the one named last changes fastest.
Arguments:
- student_img: bfloat16 [16384, 1152], P(('blk', 'narrow')), may hold values from -6 to 6
- student_txt: bfloat16 [16384, 1152], P(('blk', 'narrow')), may hold values from -6 to 6
- teacher_img: bfloat16 [16384, 1536], P(('blk', 'narrow')), may hold values from -6 to 6
- teacher_txt: bfloat16 [16384, 1536], P(('blk', 'narrow')), may hold values from -6 to 6
Outputs:
- image_grad: float32 [16384, 1152], P(('blk', 'narrow'))
- text_grad: float32 [16384, 1152], P(('blk', 'narrow'))
All inputs are finite; a program needn't handle non-finite values.
Results may differ from a plain program's by a relative error of at most 0.0097.
Values may be sent and summed in bfloat16 or wider, within the bound.
A program may use at most 128 MiB of HBM per device.

v0:
```python
import jax
import jax.numpy as jnp
from jax import lax
from jax.sharding import PartitionSpec as P

epsilon = 1e-06
logit_scale = 100.0
logit_bias = -4.0


def shifted(x, axis, by):
    count = lax.axis_size(axis)
    return lax.ppermute(x, axis, [(i, (i + by) % count) for i in range(count)])


def unit_rows(raw_rows):
    raw_float = raw_rows.astype(jnp.float32)
    radius = jnp.sqrt(jnp.sum(raw_float * raw_float, axis=1, keepdims=True) + epsilon)
    return (raw_float / radius, radius)


def unit_back(grad_unit, unit_float, radius):
    along_unit = jnp.sum(unit_float * grad_unit, axis=1, keepdims=True)
    return (grad_unit - unit_float * along_unit) / radius


def body(student_img, student_txt, teacher_img, teacher_txt):
    block_count = lax.axis_size("blk")
    block_index = lax.axis_index("blk")
    group_index = lax.axis_index("narrow")
    own_rows = student_txt.shape[0]
    embed_width = student_txt.shape[1]
    image_block, teacher_block = (
        lax.all_gather(student_img, "narrow", axis=0, tiled=True),
        lax.all_gather(teacher_img, "narrow", axis=0, tiled=True),
    )
    block_rows = image_block.shape[0]
    img_float, img_radius = unit_rows(image_block)
    img_unit = img_float.astype(jnp.bfloat16)
    t_img_unit = unit_rows(teacher_block)[0].astype(jnp.bfloat16)
    txt_float, txt_radius = unit_rows(student_txt)
    txt_unit = txt_float.astype(jnp.bfloat16)
    t_txt_unit = unit_rows(teacher_txt)[0].astype(jnp.bfloat16)
    teacher_tile = (
        logit_scale
        * jnp.einsum(
            "rd,cd->rc",
            t_img_unit,
            lax.all_gather(t_txt_unit, "blk", axis=0, tiled=True),
            preferred_element_type=jnp.float32,
        )
        + logit_bias
    )
    row_ids = lax.broadcasted_iota(jnp.int32, (block_rows, own_rows), 0)
    col_ids = lax.broadcasted_iota(jnp.int32, (block_rows, own_rows), 1) + group_index * own_rows
    same_slot = row_ids == col_ids
    pair_start = jnp.zeros((1, 1), jnp.bfloat16)

    def advance(cycle_step, cycle_state):
        text_cur, teach_cur, grad_acc, img_acc, pair_store = cycle_state
        source = (block_index - cycle_step) % block_count
        teacher_logit = lax.dynamic_slice_in_dim(teacher_tile, source * own_rows, own_rows, 1)
        student_logit = (
            logit_scale
            * jnp.einsum("rd,cd->rc", img_unit, text_cur, preferred_element_type=jnp.float32)
            + logit_bias
        )
        positive = jnp.where(same_slot & (source == block_index), 1.0, 0.0).astype(jnp.float32)
        pair_grad = (
            2.0 * jax.nn.sigmoid(student_logit) - jax.nn.sigmoid(teacher_logit) - positive
        ).astype(jnp.bfloat16)
        img_acc = img_acc + jnp.dot(pair_grad, text_cur, preferred_element_type=jnp.float32)
        grad_acc = grad_acc + jnp.einsum(
            "rc,rd->cd", pair_grad, img_unit, preferred_element_type=jnp.float32
        )
        grad_acc = shifted(grad_acc, "blk", 1)
        text_cur = shifted(text_cur, "blk", 1)
        return (text_cur, teach_cur, grad_acc, img_acc, pair_store)

    start_state = (
        txt_unit,
        t_txt_unit,
        jnp.zeros((own_rows, embed_width), jnp.float32),
        jnp.zeros((block_rows, embed_width), jnp.float32),
        pair_start,
    )
    final_state = lax.fori_loop(0, block_count, advance, start_state)
    grad_acc = final_state[2]
    img_acc = final_state[3]
    pair_store = final_state[4]
    img_grad_unit = lax.psum_scatter(
        logit_scale * img_acc, "narrow", scatter_dimension=0, tiled=True
    )
    own_float = lax.dynamic_slice_in_dim(img_float, group_index * own_rows, own_rows, 0)
    own_radius = lax.dynamic_slice_in_dim(img_radius, group_index * own_rows, own_rows, 0)
    image_grad = unit_back(img_grad_unit, own_float, own_radius)
    txt_grad_unit = logit_scale * grad_acc
    text_grad = unit_back(txt_grad_unit, txt_float, txt_radius)
    return (image_grad, text_grad)


def solution(mesh):
    in_specs = (
        P(("blk", "narrow"), None),
        P(("blk", "narrow"), None),
        P(("blk", "narrow"), None),
        P(("blk", "narrow"), None),
    )
    out_specs = (P(("blk", "narrow"), None), P(("blk", "narrow"), None))
    return jax.shard_map(body, mesh=mesh, in_specs=in_specs, out_specs=out_specs, check_vma=False)
```

profile of v0, /device:TPU:1, one launch (start us, length us, event | category | flops | bytes accessed | tf_op | source)
XLA Modules:
  0.0 579.0 jit_solution(6494705080978374956)
XLA Ops:
  14.8 34.3 %all-gather.4.cloned.1.call-done = bf16[1024,1152]{1,0:T(8,128)(2,1)} async-done(((bf16[128,1152]{1,0:T(8,128)(2,1)}), bf16[1024,1152]{1,0:T(8,128)(2,1)}) %all-gather.4.cloned.1.call-update) | async-done | bytes 2359312 | tf_op jit(solution)/shard_map/all_gather | solution.py:34
  55.8 41.1 %all-gather.6.cloned.1.call-done = bf16[1024,1536]{1,0:T(8,128)(2,1)} async-done(((bf16[128,1536]{1,0:T(8,128)(2,1)}), bf16[1024,1536]{1,0:T(8,128)(2,1)}) %all-gather.6.cloned.1.call-update) | async-done | bytes 3145744 | tf_op jit(solution)/shard_map/all_gather | solution.py:35
  99.5 66.9 %all-gather.8.cloned.1.call-done = bf16[2048,1536]{1,0:T(8,128)(2,1)} async-done(((bf16[128,1536]{1,0:T(8,128)(2,1)}), bf16[2048,1536]{1,0:T(8,128)(2,1)}) %all-gather.8.cloned.1.call-update) | async-done | bytes 6291472 | tf_op jit(solution)/shard_map/all_gather | solution.py:49
  166.3 11.8 %multiply_add_fusion = f32[1024,2048]{1,0:T(8,128)} fusion(bf16[2048,1536]{1,0:T(8,128)(2,1)} %all-gather.8.cloned.1.call-done, bf16[1024,1536]{1,0:T(8,128)(2,1)} %all-gather.6.cloned.1.call-done, f32[1024]{0:T(1024)S(1)} %add_sqrt_fusion), kind=kOutput, calls=%fused_computation.15 | convolution fusion | flops 6451363840 | bytes 17829888 | tf_op jit(solution)/shard_map/rd,cd->rc/dot_general | solution.py:46
  178.1 318.0 %while.20 = (s32[]{:T(128)}, bf16[128,1152]{1,0:T(8,128)(2,1)}, f32[128,1152]{1,0:T(8,128)S(1)}, f32[1024,1152]{1,0:T(8,128)}, bf16[1024,1152]{1,0:T(8,128)(2,1)...) while((s32[]{:T(128)}, bf16[128,1152]{1,0:T(8,128)(2,1)}, ...), condition=%wide.region_5.6_spmd.clone, body=%wide.region_4.5_spmd.clone.sunk | while | flops 910442496 | bytes 21365652 | solution.py:87
  186.1 7.0 %collective-permute-done = bf16[128,1152]{1,0:T(8,128)(2,1)} collective-permute-done((bf16[128,1152]{1,0:T(8,128)(2,1)S(1)}, bf16[128,1152]{1,0:T(8,128)(2,1)}, u32[]{:S(2)}, u32[]{:S(2)}) %collective-permute-start) | collective-permute-done | bytes 294944 | tf_op jit(solution)/shard_map/while/body/eval_jaxpr/ppermute | solution.py:13
  201.6 5.3 convolution_add_fusion.5
  258.7 5.3 convolution_add_fusion.5
  297.7 5.3 convolution_add_fusion.5
  303.0 6.5 %collective-permute-done = bf16[128,1152]{1,0:T(8,128)(2,1)} collective-permute-done((bf16[128,1152]{1,0:T(8,128)(2,1)S(1)}, bf16[128,1152]{1,0:T(8,128)(2,1)}, u32[]{:S(2)}, u32[]{:S(2)}) %collective-permute-start) | collective-permute-done | bytes 294944 | tf_op jit(solution)/shard_map/while/body/eval_jaxpr/ppermute | solution.py:13
  322.6 7.7 %collective-permute-done = bf16[128,1152]{1,0:T(8,128)(2,1)} collective-permute-done((bf16[128,1152]{1,0:T(8,128)(2,1)S(1)}, bf16[128,1152]{1,0:T(8,128)(2,1)}, u32[]{:S(2)}, u32[]{:S(2)}) %collective-permute-start) | collective-permute-done | bytes 294944 | tf_op jit(solution)/shard_map/while/body/eval_jaxpr/ppermute | solution.py:13
  336.8 5.3 convolution_add_fusion.5
  342.1 8.9 %collective-permute-done = bf16[128,1152]{1,0:T(8,128)(2,1)} collective-permute-done((bf16[128,1152]{1,0:T(8,128)(2,1)S(1)}, bf16[128,1152]{1,0:T(8,128)(2,1)}, u32[]{:S(2)}, u32[]{:S(2)}) %collective-permute-start) | collective-permute-done | bytes 294944 | tf_op jit(solution)/shard_map/while/body/eval_jaxpr/ppermute | solution.py:13
  361.6 10.1 %collective-permute-done = bf16[128,1152]{1,0:T(8,128)(2,1)} collective-permute-done((bf16[128,1152]{1,0:T(8,128)(2,1)S(1)}, bf16[128,1152]{1,0:T(8,128)(2,1)}, u32[]{:S(2)}, u32[]{:S(2)}) %collective-permute-start) | collective-permute-done | bytes 294944 | tf_op jit(solution)/shard_map/while/body/eval_jaxpr/ppermute | solution.py:13
  376.0 5.3 convolution_add_fusion.5
  381.3 11.1 %collective-permute-done = bf16[128,1152]{1,0:T(8,128)(2,1)} collective-permute-done((bf16[128,1152]{1,0:T(8,128)(2,1)S(1)}, bf16[128,1152]{1,0:T(8,128)(2,1)}, u32[]{:S(2)}, u32[]{:S(2)}) %collective-permute-start) | collective-permute-done | bytes 294944 | tf_op jit(solution)/shard_map/while/body/eval_jaxpr/ppermute | solution.py:13
  396.8 5.3 convolution_add_fusion.5
  402.1 11.1 %collective-permute-done = bf16[128,1152]{1,0:T(8,128)(2,1)} collective-permute-done((bf16[128,1152]{1,0:T(8,128)(2,1)S(1)}, bf16[128,1152]{1,0:T(8,128)(2,1)}, u32[]{:S(2)}, u32[]{:S(2)}) %collective-permute-start) | collective-permute-done | bytes 294944 | tf_op jit(solution)/shard_map/while/body/eval_jaxpr/ppermute | solution.py:13
  422.8 11.1 %collective-permute-done = bf16[128,1152]{1,0:T(8,128)(2,1)} collective-permute-done((bf16[128,1152]{1,0:T(8,128)(2,1)S(1)}, bf16[128,1152]{1,0:T(8,128)(2,1)}, u32[]{:S(2)}, u32[]{:S(2)}) %collective-permute-start) | collective-permute-done | bytes 294944 | tf_op jit(solution)/shard_map/while/body/eval_jaxpr/ppermute | solution.py:13
  438.3 5.3 convolution_add_fusion.5
  443.5 11.1 %collective-permute-done = bf16[128,1152]{1,0:T(8,128)(2,1)} collective-permute-done((bf16[128,1152]{1,0:T(8,128)(2,1)S(1)}, bf16[128,1152]{1,0:T(8,128)(2,1)}, u32[]{:S(2)}, u32[]{:S(2)}) %collective-permute-start) | collective-permute-done | bytes 294944 | tf_op jit(solution)/shard_map/while/body/eval_jaxpr/ppermute | solution.py:13
  464.3 11.1 %collective-permute-done = bf16[128,1152]{1,0:T(8,128)(2,1)} collective-permute-done((bf16[128,1152]{1,0:T(8,128)(2,1)S(1)}, bf16[128,1152]{1,0:T(8,128)(2,1)}, u32[]{:S(2)}, u32[]{:S(2)}) %collective-permute-start) | collective-permute-done | bytes 294944 | tf_op jit(solution)/shard_map/while/body/eval_jaxpr/ppermute | solution.py:13
  485.0 11.1 %collective-permute-done = bf16[128,1152]{1,0:T(8,128)(2,1)} collective-permute-done((bf16[128,1152]{1,0:T(8,128)(2,1)S(1)}, bf16[128,1152]{1,0:T(8,128)(2,1)}, u32[]{:S(2)}, u32[]{:S(2)}) %collective-permute-start) | collective-permute-done | bytes 294944 | tf_op jit(solution)/shard_map/while/body/eval_jaxpr/ppermute | solution.py:13
  503.1 65.7 %reduce-scatter.2.cloned.1.call-done = f32[128,1152]{1,0:T(8,128)} async-done(((f32[1024,1152]{1,0:T(8,128)}), f32[128,1152]{1,0:T(8,128)}) %reduce-scatter.2.cloned.1.call-update) | async-done | bytes 589840 | tf_op jit(solution)/shard_map/reduce_scatter | solution.py:91
  (140 shorter events, 201.5 us)
Async XLA Ops:
  7.2 41.9 %all-gather.4.cloned.1.call-start = ((), (), s32[]{:S(2)}) async-start(), calls=%async_computation.1 | async-start | bytes 2654208 | tf_op jit(solution)/shard_map/all_gather | solution.py:34
  7.9 89.0 %all-gather.6.cloned.1.call-start = ((), (), s32[]{:S(2)}) async-start(), calls=%async_computation.2 | async-start | bytes 3538944 | tf_op jit(solution)/shard_map/all_gather | solution.py:35
  8.6 157.7 %all-gather.8.cloned.1.call-start = ((), (), s32[]{:S(2)}) async-start(), calls=%async_computation.3 | async-start | bytes 6684672 | tf_op jit(solution)/shard_map/all_gather | solution.py:49
  11.8 557.1 %reduce-scatter.2.cloned.1.call-start = ((), (), s32[]{:S(2)}) async-start(), calls=%async_computation.4 | async-start | bytes 5308416 | tf_op jit(solution)/shard_map/reduce_scatter | solution.py:91
  272.3 16.4 %collective-permute-start.1 = (f32[128,1152]{1,0:T(8,128)}, f32[128,1152]{1,0:T(8,128)S(1)}, u32[]{:S(2)}, u32[]{:S(2)}) collective-permute-start(f32[128,1152]{1,0:T(8,128)} %convolution_add_fusion.4), channel_id=1, source_target_pairs={{0,8},{8,16},{16,24},{24,32},{32,40},{40,48},{48,56},{56,64},{64,7... | collective-permute-start | bytes 1769480 | tf_op jit(solution)/shard_map/while/body/eval_jaxpr/ppermute | solution.py:13
  293.1 16.4 %collective-permute-start.1 = (f32[128,1152]{1,0:T(8,128)}, f32[128,1152]{1,0:T(8,128)S(1)}, u32[]{:S(2)}, u32[]{:S(2)}) collective-permute-start(f32[128,1152]{1,0:T(8,128)} %convolution_add_fusion.4), channel_id=1, source_target_pairs={{0,8},{8,16},{16,24},{24,32},{32,40},{40,48},{48,56},{56,64},{64,7... | collective-permute-start | bytes 1769480 | tf_op jit(solution)/shard_map/while/body/eval_jaxpr/ppermute | solution.py:13
  313.8 16.4 %collective-permute-start.1 = (f32[128,1152]{1,0:T(8,128)}, f32[128,1152]{1,0:T(8,128)S(1)}, u32[]{:S(2)}, u32[]{:S(2)}) collective-permute-start(f32[128,1152]{1,0:T(8,128)} %convolution_add_fusion.4), channel_id=1, source_target_pairs={{0,8},{8,16},{16,24},{24,32},{32,40},{40,48},{48,56},{56,64},{64,7... | collective-permute-start | bytes 1769480 | tf_op jit(solution)/shard_map/while/body/eval_jaxpr/ppermute | solution.py:13
  313.8 16.4 %collective-permute-start = (bf16[128,1152]{1,0:T(8,128)(2,1)S(1)}, bf16[128,1152]{1,0:T(8,128)(2,1)}, u32[]{:S(2)}, u32[]{:S(2)}) collective-permute-start(bf16[128,1152]{1,0:T(8,128)(2,1)S(1)} %copy.11), channel_id=1, source_target_pairs={{0,8},{8,16},{16,24},{24,32},{32,40},{40,48},{48,56},{56,64},{64,7... | collective-permute-start | bytes 884744 | tf_op jit(solution)/shard_map/while/body/eval_jaxpr/ppermute | solution.py:13
  334.6 16.4 %collective-permute-start.1 = (f32[128,1152]{1,0:T(8,128)}, f32[128,1152]{1,0:T(8,128)S(1)}, u32[]{:S(2)}, u32[]{:S(2)}) collective-permute-start(f32[128,1152]{1,0:T(8,128)} %convolution_add_fusion.4), channel_id=1, source_target_pairs={{0,8},{8,16},{16,24},{24,32},{32,40},{40,48},{48,56},{56,64},{64,7... | collective-permute-start | bytes 1769480 | tf_op jit(solution)/shard_map/while/body/eval_jaxpr/ppermute | solution.py:13
  334.6 16.4 %collective-permute-start = (bf16[128,1152]{1,0:T(8,128)(2,1)S(1)}, bf16[128,1152]{1,0:T(8,128)(2,1)}, u32[]{:S(2)}, u32[]{:S(2)}) collective-permute-start(bf16[128,1152]{1,0:T(8,128)(2,1)S(1)} %copy.11), channel_id=1, source_target_pairs={{0,8},{8,16},{16,24},{24,32},{32,40},{40,48},{48,56},{56,64},{64,7... | collective-permute-start | bytes 884744 | tf_op jit(solution)/shard_map/while/body/eval_jaxpr/ppermute | solution.py:13
  355.3 16.4 %collective-permute-start.1 = (f32[128,1152]{1,0:T(8,128)}, f32[128,1152]{1,0:T(8,128)S(1)}, u32[]{:S(2)}, u32[]{:S(2)}) collective-permute-start(f32[128,1152]{1,0:T(8,128)} %convolution_add_fusion.4), channel_id=1, source_target_pairs={{0,8},{8,16},{16,24},{24,32},{32,40},{40,48},{48,56},{56,64},{64,7... | collective-permute-start | bytes 1769480 | tf_op jit(solution)/shard_map/while/body/eval_jaxpr/ppermute | solution.py:13
  355.3 16.4 %collective-permute-start = (bf16[128,1152]{1,0:T(8,128)(2,1)S(1)}, bf16[128,1152]{1,0:T(8,128)(2,1)}, u32[]{:S(2)}, u32[]{:S(2)}) collective-permute-start(bf16[128,1152]{1,0:T(8,128)(2,1)S(1)} %copy.11), channel_id=1, source_target_pairs={{0,8},{8,16},{16,24},{24,32},{32,40},{40,48},{48,56},{56,64},{64,7... | collective-permute-start | bytes 884744 | tf_op jit(solution)/shard_map/while/body/eval_jaxpr/ppermute | solution.py:13
  376.0 16.4 %collective-permute-start.1 = (f32[128,1152]{1,0:T(8,128)}, f32[128,1152]{1,0:T(8,128)S(1)}, u32[]{:S(2)}, u32[]{:S(2)}) collective-permute-start(f32[128,1152]{1,0:T(8,128)} %convolution_add_fusion.4), channel_id=1, source_target_pairs={{0,8},{8,16},{16,24},{24,32},{32,40},{40,48},{48,56},{56,64},{64,7... | collective-permute-start | bytes 1769480 | tf_op jit(solution)/shard_map/while/body/eval_jaxpr/ppermute | solution.py:13
  376.0 16.4 %collective-permute-start = (bf16[128,1152]{1,0:T(8,128)(2,1)S(1)}, bf16[128,1152]{1,0:T(8,128)(2,1)}, u32[]{:S(2)}, u32[]{:S(2)}) collective-permute-start(bf16[128,1152]{1,0:T(8,128)(2,1)S(1)} %copy.11), channel_id=1, source_target_pairs={{0,8},{8,16},{16,24},{24,32},{32,40},{40,48},{48,56},{56,64},{64,7... | collective-permute-start | bytes 884744 | tf_op jit(solution)/shard_map/while/body/eval_jaxpr/ppermute | solution.py:13
  396.8 16.4 %collective-permute-start.1 = (f32[128,1152]{1,0:T(8,128)}, f32[128,1152]{1,0:T(8,128)S(1)}, u32[]{:S(2)}, u32[]{:S(2)}) collective-permute-start(f32[128,1152]{1,0:T(8,128)} %convolution_add_fusion.4), channel_id=1, source_target_pairs={{0,8},{8,16},{16,24},{24,32},{32,40},{40,48},{48,56},{56,64},{64,7... | collective-permute-start | bytes 1769480 | tf_op jit(solution)/shard_map/while/body/eval_jaxpr/ppermute | solution.py:13
  396.8 16.4 %collective-permute-start = (bf16[128,1152]{1,0:T(8,128)(2,1)S(1)}, bf16[128,1152]{1,0:T(8,128)(2,1)}, u32[]{:S(2)}, u32[]{:S(2)}) collective-permute-start(bf16[128,1152]{1,0:T(8,128)(2,1)S(1)} %copy.11), channel_id=1, source_target_pairs={{0,8},{8,16},{16,24},{24,32},{32,40},{40,48},{48,56},{56,64},{64,7... | collective-permute-start | bytes 884744 | tf_op jit(solution)/shard_map/while/body/eval_jaxpr/ppermute | solution.py:13
  417.5 16.4 %collective-permute-start.1 = (f32[128,1152]{1,0:T(8,128)}, f32[128,1152]{1,0:T(8,128)S(1)}, u32[]{:S(2)}, u32[]{:S(2)}) collective-permute-start(f32[128,1152]{1,0:T(8,128)} %convolution_add_fusion.4), channel_id=1, source_target_pairs={{0,8},{8,16},{16,24},{24,32},{32,40},{40,48},{48,56},{56,64},{64,7... | collective-permute-start | bytes 1769480 | tf_op jit(solution)/shard_map/while/body/eval_jaxpr/ppermute | solution.py:13
  417.5 16.4 %collective-permute-start = (bf16[128,1152]{1,0:T(8,128)(2,1)S(1)}, bf16[128,1152]{1,0:T(8,128)(2,1)}, u32[]{:S(2)}, u32[]{:S(2)}) collective-permute-start(bf16[128,1152]{1,0:T(8,128)(2,1)S(1)} %copy.11), channel_id=1, source_target_pairs={{0,8},{8,16},{16,24},{24,32},{32,40},{40,48},{48,56},{56,64},{64,7... | collective-permute-start | bytes 884744 | tf_op jit(solution)/shard_map/while/body/eval_jaxpr/ppermute | solution.py:13
  438.3 16.4 %collective-permute-start.1 = (f32[128,1152]{1,0:T(8,128)}, f32[128,1152]{1,0:T(8,128)S(1)}, u32[]{:S(2)}, u32[]{:S(2)}) collective-permute-start(f32[128,1152]{1,0:T(8,128)} %convolution_add_fusion.4), channel_id=1, source_target_pairs={{0,8},{8,16},{16,24},{24,32},{32,40},{40,48},{48,56},{56,64},{64,7... | collective-permute-start | bytes 1769480 | tf_op jit(solution)/shard_map/while/body/eval_jaxpr/ppermute | solution.py:13
  438.3 16.4 %collective-permute-start = (bf16[128,1152]{1,0:T(8,128)(2,1)S(1)}, bf16[128,1152]{1,0:T(8,128)(2,1)}, u32[]{:S(2)}, u32[]{:S(2)}) collective-permute-start(bf16[128,1152]{1,0:T(8,128)(2,1)S(1)} %copy.11), channel_id=1, source_target_pairs={{0,8},{8,16},{16,24},{24,32},{32,40},{40,48},{48,56},{56,64},{64,7... | collective-permute-start | bytes 884744 | tf_op jit(solution)/shard_map/while/body/eval_jaxpr/ppermute | solution.py:13
  459.0 16.4 %collective-permute-start.1 = (f32[128,1152]{1,0:T(8,128)}, f32[128,1152]{1,0:T(8,128)S(1)}, u32[]{:S(2)}, u32[]{:S(2)}) collective-permute-start(f32[128,1152]{1,0:T(8,128)} %convolution_add_fusion.4), channel_id=1, source_target_pairs={{0,8},{8,16},{16,24},{24,32},{32,40},{40,48},{48,56},{56,64},{64,7... | collective-permute-start | bytes 1769480 | tf_op jit(solution)/shard_map/while/body/eval_jaxpr/ppermute | solution.py:13
  459.0 16.4 %collective-permute-start = (bf16[128,1152]{1,0:T(8,128)(2,1)S(1)}, bf16[128,1152]{1,0:T(8,128)(2,1)}, u32[]{:S(2)}, u32[]{:S(2)}) collective-permute-start(bf16[128,1152]{1,0:T(8,128)(2,1)S(1)} %copy.11), channel_id=1, source_target_pairs={{0,8},{8,16},{16,24},{24,32},{32,40},{40,48},{48,56},{56,64},{64,7... | collective-permute-start | bytes 884744 | tf_op jit(solution)/shard_map/while/body/eval_jaxpr/ppermute | solution.py:13
  479.7 16.4 %collective-permute-start.1 = (f32[128,1152]{1,0:T(8,128)}, f32[128,1152]{1,0:T(8,128)S(1)}, u32[]{:S(2)}, u32[]{:S(2)}) collective-permute-start(f32[128,1152]{1,0:T(8,128)} %convolution_add_fusion.4), channel_id=1, source_target_pairs={{0,8},{8,16},{16,24},{24,32},{32,40},{40,48},{48,56},{56,64},{64,7... | collective-permute-start | bytes 1769480 | tf_op jit(solution)/shard_map/while/body/eval_jaxpr/ppermute | solution.py:13
  479.7 16.4 %collective-permute-start = (bf16[128,1152]{1,0:T(8,128)(2,1)S(1)}, bf16[128,1152]{1,0:T(8,128)(2,1)}, u32[]{:S(2)}, u32[]{:S(2)}) collective-permute-start(bf16[128,1152]{1,0:T(8,128)(2,1)S(1)} %copy.11), channel_id=1, source_target_pairs={{0,8},{8,16},{16,24},{24,32},{32,40},{40,48},{48,56},{56,64},{64,7... | collective-permute-start | bytes 884744 | tf_op jit(solution)/shard_map/while/body/eval_jaxpr/ppermute | solution.py:13
  (13 other events, 147.9 us)
Sparse Core Ops, SparseCore 0:
  9.6 39.4 all-gather.3
  50.7 46.1 all-gather.5
  99.9 66.3 all-gather.7
  501.1 67.7 reduce-scatter.1
where the time goes:
time: 581 us; the launch traced here: 579 us
  waiting for transfers between devices  340 us (59%)
  matrix products  148 us (25%)
  starting transfers between devices  36.1 us (6%)
  other arithmetic  24.9 us (4%)
  local copies, waits for them, and re-layouts  16.4 us (3%)
  between operations  13.8 us (2%)
    ppermute x32, waiting for transfers between devices, shifted(): return lax.ppermute(x, axis, [(i, (i + by) % count) for i in range(count)])  130 us
    dot_general x16, matrix products, advance(): jnp.dot(pair_grad, text_cur, preferred_element_type=jnp.float32)  82.2 us
    all_gather x1, waiting for transfers between devices, body(): lax.all_gather(t_txt_unit, 'blk', axis=0, tiled=True)  66.9 us
    reduce_scatter x1, waiting for transfers between devices, body(): lax.psum_scatter(logit_scale * img_acc, 'narrow', scatter_dimension=0, ti...  65.7 us
    all_gather x1, waiting for transfers between devices, body(): lax.all_gather(teacher_img, 'narrow', axis=0, tiled=True)  41.1 us
    ppermute x32, starting transfers between devices, shifted(): return lax.ppermute(x, axis, [(i, (i + by) % count) for i in range(count)])  36 us
    all_gather x1, waiting for transfers between devices, body(): lax.all_gather(student_img, 'narrow', axis=0, tiled=True)  34.3 us
    dot_general x16, matrix products, advance(): jnp.einsum('rd,cd->rc', img_unit, text_cur, preferred_element_type=jnp.fl...  32.1 us
  transfers between devices with their start and end apart: 36, of which 20 were waited for; matrix products, arithmetic and copies ran while one was open for 17% of the time, Pallas kernels for 0%

commit v1 on v0

--- a/solution.py
+++ b/solution.py
@@ -6,6 +6,11 @@
 epsilon = 1e-06
 logit_scale = 100.0
 logit_bias = -4.0
+
+
+def swapped_in(value, axis, along):
+    sent = jnp.stack([value] * lax.axis_size(axis))
+    return jnp.concatenate(lax.all_to_all(sent, axis, 0, 0), axis=along)
 
 
 def shifted(x, axis, by):
@@ -46,7 +51,7 @@
         * jnp.einsum(
             "rd,cd->rc",
             t_img_unit,
-            lax.all_gather(t_txt_unit, "blk", axis=0, tiled=True),
+            swapped_in(t_txt_unit, "blk", 0),
             preferred_element_type=jnp.float32,
         )
         + logit_bias

time: 581 us -> 561 us (0.966)
  waiting for transfers between devices: 340 us -> 313 us
  starting transfers between devices: 36.1 us -> 42.6 us
    all_gather x1 -> x0, waiting for transfers between devices: 66.9 us -> none  [body(): lax.all_gather(t_txt_unit, 'blk', axis=0, tiled=True)]
    all_gather x1, waiting for transfers between devices: 41.1 us -> 67.6 us  [body(): lax.all_gather(teacher_img, 'narrow', axis=0, tiled=True)]
    all_to_all x0 -> x1, starting transfers between devices: none -> 9.41 us  [swapped_in(): return jnp.concatenate(lax.all_to_all(sent, axis, 0, 0), axis=along)]
    all_gather x1, waiting for transfers between devices: 34.3 us -> 42.8 us  [body(): lax.all_gather(student_img, 'narrow', axis=0, tiled=True)]
  transfers between devices with their start and end apart: 36 -> 36, of which waited for: 20 -> 20; matrix products, arithmetic and copies ran while one was open for 17% -> 18% of each run, Pallas kernels for 0% -> 0%
where the time goes in v1:
time: 561 us; the launch traced here: 559 us
  waiting for transfers between devices  313 us (56%)
  matrix products  148 us (26%)
  starting transfers between devices  42.6 us (8%)
  other arithmetic  22.2 us (4%)
  local copies, waits for them, and re-layouts  19.7 us (4%)
  between operations  13.8 us (2%)
    ppermute x32, waiting for transfers between devices, shifted(): return lax.ppermute(x, axis, [(i, (i + by) % count) for i in range(count)])  134 us
    dot_general x16, matrix products, advance(): jnp.dot(pair_grad, text_cur, preferred_element_type=jnp.float32)  82.2 us
    all_gather x1, waiting for transfers between devices, body(): lax.all_gather(teacher_img, 'narrow', axis=0, tiled=True)  67.6 us
    reduce_scatter x1, waiting for transfers between devices, body(): lax.psum_scatter(logit_scale * img_acc, 'narrow', scatter_dimension=0, ti...  65.4 us
    all_gather x1, waiting for transfers between devices, body(): lax.all_gather(student_img, 'narrow', axis=0, tiled=True)  42.8 us
    ppermute x32, starting transfers between devices, shifted(): return lax.ppermute(x, axis, [(i, (i + by) % count) for i in range(count)])  33 us
    dot_general x16, matrix products, advance(): jnp.einsum('rd,cd->rc', img_unit, text_cur, preferred_element_type=jnp.fl...  32.1 us
    dot_general x16, matrix products, advance(): jnp.einsum('rc,rd->cd', pair_grad, img_unit, preferred_element_type=jnp.f...  21.8 us
  transfers between devices with their start and end apart: 36, of which 20 were waited for; matrix products, arithmetic and copies ran while one was open for 18% of the time, Pallas kernels for 0%

profile of v1, /device:TPU:1, one launch (start us, length us, event | category | flops | bytes accessed | tf_op | source)
XLA Modules:
  0.0 559.0 jit_solution(9135489168293927808)
XLA Ops:
  14.2 9.4 %all-to-all-start = ((bf16[16,128,1536]{2,1,0:T(8,128)(2,1)}), bf16[16,128,1536]{2,1,0:T(8,128)(2,1)}, u32[]{:S(2)}, u32[]{:S(2)}) async-start(bf16[16,128,1536]{2,1,0:T(8,128)(2,1)} %stack.2), calls=%async_computation | async-start | bytes 12582912 | tf_op jit(solution)/shard_map/all_to_all | solution.py:13
  24.7 42.8 %all-gather.3.cloned.1.call-done = bf16[1024,1152]{1,0:T(8,128)(2,1)} async-done(((bf16[128,1152]{1,0:T(8,128)(2,1)}), bf16[1024,1152]{1,0:T(8,128)(2,1)}) %all-gather.3.cloned.1.call-update) | async-done | bytes 2359312 | tf_op jit(solution)/shard_map/all_gather | solution.py:39
  74.2 67.6 %all-gather.5.cloned.1.call-done = bf16[1024,1536]{1,0:T(8,128)(2,1)} async-done(((bf16[128,1536]{1,0:T(8,128)(2,1)}), bf16[1024,1536]{1,0:T(8,128)(2,1)}) %all-gather.5.cloned.1.call-update) | async-done | bytes 3145744 | tf_op jit(solution)/shard_map/all_gather | solution.py:40
  146.4 11.8 %multiply_add_fusion = f32[1024,2048]{1,0:T(8,128)} fusion(bf16[2048,1536]{1,0:T(8,128)(2,1)} %bitcast, bf16[1024,1536]{1,0:T(8,128)(2,1)} %all-gather.5.cloned.1.call-done, f32[1024]{0:T(1024)S(1)} %add_sqrt_fusion), kind=kOutput, calls=%fused_computation.15 | convolution fusion | flops 6451363840 | bytes 17829888 | tf_op jit(solution)/shard_map/rd,cd->rc/dot_general | solution.py:51
  158.2 318.4 %while.20 = (s32[]{:T(128)}, bf16[128,1152]{1,0:T(8,128)(2,1)}, f32[128,1152]{1,0:T(8,128)S(1)}, f32[1024,1152]{1,0:T(8,128)}, bf16[1024,1152]{1,0:T(8,128)(2,1)...) while((s32[]{:T(128)}, bf16[128,1152]{1,0:T(8,128)(2,1)}, ...), condition=%wide.region_5.6_spmd.clone, body=%wide.region_4.5_spmd.clone.sunk | while | flops 910442496 | bytes 21365652 | solution.py:92
  166.5 7.2 %collective-permute-done = bf16[128,1152]{1,0:T(8,128)(2,1)} collective-permute-done((bf16[128,1152]{1,0:T(8,128)(2,1)S(1)}, bf16[128,1152]{1,0:T(8,128)(2,1)}, u32[]{:S(2)}, u32[]{:S(2)}) %collective-permute-start) | collective-permute-done | bytes 294944 | tf_op jit(solution)/shard_map/while/body/eval_jaxpr/ppermute | solution.py:18
  238.6 5.3 convolution_add_fusion.5
  263.4 5.7 %collective-permute-done = bf16[128,1152]{1,0:T(8,128)(2,1)} collective-permute-done((bf16[128,1152]{1,0:T(8,128)(2,1)S(1)}, bf16[128,1152]{1,0:T(8,128)(2,1)}, u32[]{:S(2)}, u32[]{:S(2)}) %collective-permute-start) | collective-permute-done | bytes 294944 | tf_op jit(solution)/shard_map/while/body/eval_jaxpr/ppermute | solution.py:18
  277.7 5.3 convolution_add_fusion.5
  283.0 6.9 %collective-permute-done = bf16[128,1152]{1,0:T(8,128)(2,1)} collective-permute-done((bf16[128,1152]{1,0:T(8,128)(2,1)S(1)}, bf16[128,1152]{1,0:T(8,128)(2,1)}, u32[]{:S(2)}, u32[]{:S(2)}) %collective-permute-start) | collective-permute-done | bytes 294944 | tf_op jit(solution)/shard_map/while/body/eval_jaxpr/ppermute | solution.py:18
  302.5 8.1 %collective-permute-done = bf16[128,1152]{1,0:T(8,128)(2,1)} collective-permute-done((bf16[128,1152]{1,0:T(8,128)(2,1)S(1)}, bf16[128,1152]{1,0:T(8,128)(2,1)}, u32[]{:S(2)}, u32[]{:S(2)}) %collective-permute-start) | collective-permute-done | bytes 294944 | tf_op jit(solution)/shard_map/while/body/eval_jaxpr/ppermute | solution.py:18
  316.7 5.3 convolution_add_fusion.5
  322.0 9.3 %collective-permute-done = bf16[128,1152]{1,0:T(8,128)(2,1)} collective-permute-done((bf16[128,1152]{1,0:T(8,128)(2,1)S(1)}, bf16[128,1152]{1,0:T(8,128)(2,1)}, u32[]{:S(2)}, u32[]{:S(2)}) %collective-permute-start) | collective-permute-done | bytes 294944 | tf_op jit(solution)/shard_map/while/body/eval_jaxpr/ppermute | solution.py:18
  341.5 10.6 %collective-permute-done = bf16[128,1152]{1,0:T(8,128)(2,1)} collective-permute-done((bf16[128,1152]{1,0:T(8,128)(2,1)S(1)}, bf16[128,1152]{1,0:T(8,128)(2,1)}, u32[]{:S(2)}, u32[]{:S(2)}) %collective-permute-start) | collective-permute-done | bytes 294944 | tf_op jit(solution)/shard_map/while/body/eval_jaxpr/ppermute | solution.py:18
  356.4 5.3 convolution_add_fusion.5
  361.7 11.1 %collective-permute-done = bf16[128,1152]{1,0:T(8,128)(2,1)} collective-permute-done((bf16[128,1152]{1,0:T(8,128)(2,1)S(1)}, bf16[128,1152]{1,0:T(8,128)(2,1)}, u32[]{:S(2)}, u32[]{:S(2)}) %collective-permute-start) | collective-permute-done | bytes 294944 | tf_op jit(solution)/shard_map/while/body/eval_jaxpr/ppermute | solution.py:18
  377.2 5.3 convolution_add_fusion.5
  382.4 11.1 %collective-permute-done = bf16[128,1152]{1,0:T(8,128)(2,1)} collective-permute-done((bf16[128,1152]{1,0:T(8,128)(2,1)S(1)}, bf16[128,1152]{1,0:T(8,128)(2,1)}, u32[]{:S(2)}, u32[]{:S(2)}) %collective-permute-start) | collective-permute-done | bytes 294944 | tf_op jit(solution)/shard_map/while/body/eval_jaxpr/ppermute | solution.py:18
  403.2 11.1 %collective-permute-done = bf16[128,1152]{1,0:T(8,128)(2,1)} collective-permute-done((bf16[128,1152]{1,0:T(8,128)(2,1)S(1)}, bf16[128,1152]{1,0:T(8,128)(2,1)}, u32[]{:S(2)}, u32[]{:S(2)}) %collective-permute-start) | collective-permute-done | bytes 294944 | tf_op jit(solution)/shard_map/while/body/eval_jaxpr/ppermute | solution.py:18
  423.9 11.1 %collective-permute-done = bf16[128,1152]{1,0:T(8,128)(2,1)} collective-permute-done((bf16[128,1152]{1,0:T(8,128)(2,1)S(1)}, bf16[128,1152]{1,0:T(8,128)(2,1)}, u32[]{:S(2)}, u32[]{:S(2)}) %collective-permute-start) | collective-permute-done | bytes 294944 | tf_op jit(solution)/shard_map/while/body/eval_jaxpr/ppermute | solution.py:18
  439.4 5.3 convolution_add_fusion.5
  444.7 11.1 %collective-permute-done = bf16[128,1152]{1,0:T(8,128)(2,1)} collective-permute-done((bf16[128,1152]{1,0:T(8,128)(2,1)S(1)}, bf16[128,1152]{1,0:T(8,128)(2,1)}, u32[]{:S(2)}, u32[]{:S(2)}) %collective-permute-start) | collective-permute-done | bytes 294944 | tf_op jit(solution)/shard_map/while/body/eval_jaxpr/ppermute | solution.py:18
  465.4 11.1 %collective-permute-done = bf16[128,1152]{1,0:T(8,128)(2,1)} collective-permute-done((bf16[128,1152]{1,0:T(8,128)(2,1)S(1)}, bf16[128,1152]{1,0:T(8,128)(2,1)}, u32[]{:S(2)}, u32[]{:S(2)}) %collective-permute-start) | collective-permute-done | bytes 294944 | tf_op jit(solution)/shard_map/while/body/eval_jaxpr/ppermute | solution.py:18
  483.5 65.4 %reduce-scatter.2.cloned.1.call-done = f32[128,1152]{1,0:T(8,128)} async-done(((f32[1024,1152]{1,0:T(8,128)}), f32[128,1152]{1,0:T(8,128)}) %reduce-scatter.2.cloned.1.call-update) | async-done | bytes 589840 | tf_op jit(solution)/shard_map/reduce_scatter | solution.py:96
  (142 shorter events, 201.9 us)
Async XLA Ops:
  7.2 60.3 %all-gather.3.cloned.1.call-start = ((), (), s32[]{:S(2)}) async-start(), calls=%async_computation.2 | async-start | bytes 2654208 | tf_op jit(solution)/shard_map/all_gather | solution.py:39
  7.9 133.9 %all-gather.5.cloned.1.call-start = ((), (), s32[]{:S(2)}) async-start(), calls=%async_computation.3 | async-start | bytes 3538944 | tf_op jit(solution)/shard_map/all_gather | solution.py:40
  14.2 132.2 %all-to-all-start = ((bf16[16,128,1536]{2,1,0:T(8,128)(2,1)}), bf16[16,128,1536]{2,1,0:T(8,128)(2,1)}, u32[]{:S(2)}, u32[]{:S(2)}) async-start(bf16[16,128,1536]{2,1,0:T(8,128)(2,1)} %stack.2), calls=%async_computation | async-start | bytes 12582912 | tf_op jit(solution)/shard_map/all_to_all | solution.py:13
  23.6 525.3 %reduce-scatter.2.cloned.1.call-start = ((), (), s32[]{:S(2)}) async-start(), calls=%async_computation.4 | async-start | bytes 5308416 | tf_op jit(solution)/shard_map/reduce_scatter | solution.py:96
  252.7 16.4 %collective-permute-start.1 = (f32[128,1152]{1,0:T(8,128)}, f32[128,1152]{1,0:T(8,128)S(1)}, u32[]{:S(2)}, u32[]{:S(2)}) collective-permute-start(f32[128,1152]{1,0:T(8,128)} %convolution_add_fusion.4), channel_id=1, source_target_pairs={{0,8},{8,16},{16,24},{24,32},{32,40},{40,48},{48,56},{56,64},{64,7... | collective-permute-start | bytes 1769480 | tf_op jit(solution)/shard_map/while/body/eval_jaxpr/ppermute | solution.py:18
  273.5 16.4 %collective-permute-start.1 = (f32[128,1152]{1,0:T(8,128)}, f32[128,1152]{1,0:T(8,128)S(1)}, u32[]{:S(2)}, u32[]{:S(2)}) collective-permute-start(f32[128,1152]{1,0:T(8,128)} %convolution_add_fusion.4), channel_id=1, source_target_pairs={{0,8},{8,16},{16,24},{24,32},{32,40},{40,48},{48,56},{56,64},{64,7... | collective-permute-start | bytes 1769480 | tf_op jit(solution)/shard_map/while/body/eval_jaxpr/ppermute | solution.py:18
  294.2 16.4 %collective-permute-start.1 = (f32[128,1152]{1,0:T(8,128)}, f32[128,1152]{1,0:T(8,128)S(1)}, u32[]{:S(2)}, u32[]{:S(2)}) collective-permute-start(f32[128,1152]{1,0:T(8,128)} %convolution_add_fusion.4), channel_id=1, source_target_pairs={{0,8},{8,16},{16,24},{24,32},{32,40},{40,48},{48,56},{56,64},{64,7... | collective-permute-start | bytes 1769480 | tf_op jit(solution)/shard_map/while/body/eval_jaxpr/ppermute | solution.py:18
  294.2 16.4 %collective-permute-start = (bf16[128,1152]{1,0:T(8,128)(2,1)S(1)}, bf16[128,1152]{1,0:T(8,128)(2,1)}, u32[]{:S(2)}, u32[]{:S(2)}) collective-permute-start(bf16[128,1152]{1,0:T(8,128)(2,1)S(1)} %copy.11), channel_id=1, source_target_pairs={{0,8},{8,16},{16,24},{24,32},{32,40},{40,48},{48,56},{56,64},{64,7... | collective-permute-start | bytes 884744 | tf_op jit(solution)/shard_map/while/body/eval_jaxpr/ppermute | solution.py:18
  314.9 16.4 %collective-permute-start.1 = (f32[128,1152]{1,0:T(8,128)}, f32[128,1152]{1,0:T(8,128)S(1)}, u32[]{:S(2)}, u32[]{:S(2)}) collective-permute-start(f32[128,1152]{1,0:T(8,128)} %convolution_add_fusion.4), channel_id=1, source_target_pairs={{0,8},{8,16},{16,24},{24,32},{32,40},{40,48},{48,56},{56,64},{64,7... | collective-permute-start | bytes 1769480 | tf_op jit(solution)/shard_map/while/body/eval_jaxpr/ppermute | solution.py:18
  314.9 16.4 %collective-permute-start = (bf16[128,1152]{1,0:T(8,128)(2,1)S(1)}, bf16[128,1152]{1,0:T(8,128)(2,1)}, u32[]{:S(2)}, u32[]{:S(2)}) collective-permute-start(bf16[128,1152]{1,0:T(8,128)(2,1)S(1)} %copy.11), channel_id=1, source_target_pairs={{0,8},{8,16},{16,24},{24,32},{32,40},{40,48},{48,56},{56,64},{64,7... | collective-permute-start | bytes 884744 | tf_op jit(solution)/shard_map/while/body/eval_jaxpr/ppermute | solution.py:18
  335.7 16.4 %collective-permute-start.1 = (f32[128,1152]{1,0:T(8,128)}, f32[128,1152]{1,0:T(8,128)S(1)}, u32[]{:S(2)}, u32[]{:S(2)}) collective-permute-start(f32[128,1152]{1,0:T(8,128)} %convolution_add_fusion.4), channel_id=1, source_target_pairs={{0,8},{8,16},{16,24},{24,32},{32,40},{40,48},{48,56},{56,64},{64,7... | collective-permute-start | bytes 1769480 | tf_op jit(solution)/shard_map/while/body/eval_jaxpr/ppermute | solution.py:18
  335.7 16.4 %collective-permute-start = (bf16[128,1152]{1,0:T(8,128)(2,1)S(1)}, bf16[128,1152]{1,0:T(8,128)(2,1)}, u32[]{:S(2)}, u32[]{:S(2)}) collective-permute-start(bf16[128,1152]{1,0:T(8,128)(2,1)S(1)} %copy.11), channel_id=1, source_target_pairs={{0,8},{8,16},{16,24},{24,32},{32,40},{40,48},{48,56},{56,64},{64,7... | collective-permute-start | bytes 884744 | tf_op jit(solution)/shard_map/while/body/eval_jaxpr/ppermute | solution.py:18
  356.4 16.4 %collective-permute-start.1 = (f32[128,1152]{1,0:T(8,128)}, f32[128,1152]{1,0:T(8,128)S(1)}, u32[]{:S(2)}, u32[]{:S(2)}) collective-permute-start(f32[128,1152]{1,0:T(8,128)} %convolution_add_fusion.4), channel_id=1, source_target_pairs={{0,8},{8,16},{16,24},{24,32},{32,40},{40,48},{48,56},{56,64},{64,7... | collective-permute-start | bytes 1769480 | tf_op jit(solution)/shard_map/while/body/eval_jaxpr/ppermute | solution.py:18
  356.4 16.4 %collective-permute-start = (bf16[128,1152]{1,0:T(8,128)(2,1)S(1)}, bf16[128,1152]{1,0:T(8,128)(2,1)}, u32[]{:S(2)}, u32[]{:S(2)}) collective-permute-start(bf16[128,1152]{1,0:T(8,128)(2,1)S(1)} %copy.11), channel_id=1, source_target_pairs={{0,8},{8,16},{16,24},{24,32},{32,40},{40,48},{48,56},{56,64},{64,7... | collective-permute-start | bytes 884744 | tf_op jit(solution)/shard_map/while/body/eval_jaxpr/ppermute | solution.py:18
  377.2 16.4 %collective-permute-start.1 = (f32[128,1152]{1,0:T(8,128)}, f32[128,1152]{1,0:T(8,128)S(1)}, u32[]{:S(2)}, u32[]{:S(2)}) collective-permute-start(f32[128,1152]{1,0:T(8,128)} %convolution_add_fusion.4), channel_id=1, source_target_pairs={{0,8},{8,16},{16,24},{24,32},{32,40},{40,48},{48,56},{56,64},{64,7... | collective-permute-start | bytes 1769480 | tf_op jit(solution)/shard_map/while/body/eval_jaxpr/ppermute | solution.py:18
  377.2 16.4 %collective-permute-start = (bf16[128,1152]{1,0:T(8,128)(2,1)S(1)}, bf16[128,1152]{1,0:T(8,128)(2,1)}, u32[]{:S(2)}, u32[]{:S(2)}) collective-permute-start(bf16[128,1152]{1,0:T(8,128)(2,1)S(1)} %copy.11), channel_id=1, source_target_pairs={{0,8},{8,16},{16,24},{24,32},{32,40},{40,48},{48,56},{56,64},{64,7... | collective-permute-start | bytes 884744 | tf_op jit(solution)/shard_map/while/body/eval_jaxpr/ppermute | solution.py:18
  397.9 16.4 %collective-permute-start.1 = (f32[128,1152]{1,0:T(8,128)}, f32[128,1152]{1,0:T(8,128)S(1)}, u32[]{:S(2)}, u32[]{:S(2)}) collective-permute-start(f32[128,1152]{1,0:T(8,128)} %convolution_add_fusion.4), channel_id=1, source_target_pairs={{0,8},{8,16},{16,24},{24,32},{32,40},{40,48},{48,56},{56,64},{64,7... | collective-permute-start | bytes 1769480 | tf_op jit(solution)/shard_map/while/body/eval_jaxpr/ppermute | solution.py:18
  397.9 16.4 %collective-permute-start = (bf16[128,1152]{1,0:T(8,128)(2,1)S(1)}, bf16[128,1152]{1,0:T(8,128)(2,1)}, u32[]{:S(2)}, u32[]{:S(2)}) collective-permute-start(bf16[128,1152]{1,0:T(8,128)(2,1)S(1)} %copy.11), channel_id=1, source_target_pairs={{0,8},{8,16},{16,24},{24,32},{32,40},{40,48},{48,56},{56,64},{64,7... | collective-permute-start | bytes 884744 | tf_op jit(solution)/shard_map/while/body/eval_jaxpr/ppermute | solution.py:18
  418.6 16.4 %collective-permute-start.1 = (f32[128,1152]{1,0:T(8,128)}, f32[128,1152]{1,0:T(8,128)S(1)}, u32[]{:S(2)}, u32[]{:S(2)}) collective-permute-start(f32[128,1152]{1,0:T(8,128)} %convolution_add_fusion.4), channel_id=1, source_target_pairs={{0,8},{8,16},{16,24},{24,32},{32,40},{40,48},{48,56},{56,64},{64,7... | collective-permute-start | bytes 1769480 | tf_op jit(solution)/shard_map/while/body/eval_jaxpr/ppermute | solution.py:18
  418.6 16.4 %collective-permute-start = (bf16[128,1152]{1,0:T(8,128)(2,1)S(1)}, bf16[128,1152]{1,0:T(8,128)(2,1)}, u32[]{:S(2)}, u32[]{:S(2)}) collective-permute-start(bf16[128,1152]{1,0:T(8,128)(2,1)S(1)} %copy.11), channel_id=1, source_target_pairs={{0,8},{8,16},{16,24},{24,32},{32,40},{40,48},{48,56},{56,64},{64,7... | collective-permute-start | bytes 884744 | tf_op jit(solution)/shard_map/while/body/eval_jaxpr/ppermute | solution.py:18
  439.4 16.4 %collective-permute-start.1 = (f32[128,1152]{1,0:T(8,128)}, f32[128,1152]{1,0:T(8,128)S(1)}, u32[]{:S(2)}, u32[]{:S(2)}) collective-permute-start(f32[128,1152]{1,0:T(8,128)} %convolution_add_fusion.4), channel_id=1, source_target_pairs={{0,8},{8,16},{16,24},{24,32},{32,40},{40,48},{48,56},{56,64},{64,7... | collective-permute-start | bytes 1769480 | tf_op jit(solution)/shard_map/while/body/eval_jaxpr/ppermute | solution.py:18
  439.4 16.4 %collective-permute-start = (bf16[128,1152]{1,0:T(8,128)(2,1)S(1)}, bf16[128,1152]{1,0:T(8,128)(2,1)}, u32[]{:S(2)}, u32[]{:S(2)}) collective-permute-start(bf16[128,1152]{1,0:T(8,128)(2,1)S(1)} %copy.11), channel_id=1, source_target_pairs={{0,8},{8,16},{16,24},{24,32},{32,40},{40,48},{48,56},{56,64},{64,7... | collective-permute-start | bytes 884744 | tf_op jit(solution)/shard_map/while/body/eval_jaxpr/ppermute | solution.py:18
  460.1 16.4 %collective-permute-start.1 = (f32[128,1152]{1,0:T(8,128)}, f32[128,1152]{1,0:T(8,128)S(1)}, u32[]{:S(2)}, u32[]{:S(2)}) collective-permute-start(f32[128,1152]{1,0:T(8,128)} %convolution_add_fusion.4), channel_id=1, source_target_pairs={{0,8},{8,16},{16,24},{24,32},{32,40},{40,48},{48,56},{56,64},{64,7... | collective-permute-start | bytes 1769480 | tf_op jit(solution)/shard_map/while/body/eval_jaxpr/ppermute | solution.py:18
  460.1 16.4 %collective-permute-start = (bf16[128,1152]{1,0:T(8,128)(2,1)S(1)}, bf16[128,1152]{1,0:T(8,128)(2,1)}, u32[]{:S(2)}, u32[]{:S(2)}) collective-permute-start(bf16[128,1152]{1,0:T(8,128)(2,1)S(1)} %copy.11), channel_id=1, source_target_pairs={{0,8},{8,16},{16,24},{24,32},{32,40},{40,48},{48,56},{56,64},{64,7... | collective-permute-start | bytes 884744 | tf_op jit(solution)/shard_map/while/body/eval_jaxpr/ppermute | solution.py:18
  (14 other events, 157.0 us)
Sparse Core Ops, SparseCore 0:
  9.6 57.8 all-gather.2
  69.1 72.6 all-gather.4
  481.4 67.4 reduce-scatter.1
